TPU v7x, 128 devices: a whole 4x4x4 slice. The times are simulated.
128 devices in a mesh: gx: 4 (over y), gy: 4 (over x_lo, core), gz: 8 (over x_hi, z).
Axes of the slice: x: 4 (x_hi: 2, x_lo: 2; x = x_hi * 2 + x_lo), y: 4, z: 4, core: 2. Of those that a mesh axis runs over, the one named last changes fastest.
Arguments:
- inputs: bfloat16 [112, 112, 56, 96], P('gx', 'gy', 'gz'), may hold values from -6 to 6
- d_out: bfloat16 [112, 112, 56, 96], P('gx', 'gy', 'gz'), may hold values from -6 to 6
- layer_norm_gain: float32 [96], replicated, may hold values from 0.1 to 1.9
- layer_norm_bias: float32 [96], replicated, may hold values from -3 to 3
- w_qkv: bfloat16 [96, 288], replicated, may hold values from -0.625 to 0.625
- b_qkv: float32 [288], replicated, may hold values from -3 to 3
- w_proj: bfloat16 [96, 96], replicated, may hold values from -0.625 to 0.625
- rel_bias: float32 [3, 2197], replicated, may hold values from -4 to 240
Outputs:
- d_x: bfloat16 [112, 112, 56, 96], P('gx', 'gy', 'gz')
- g_qkv: float32 [96, 288], replicated
- g_bqkv: float32 [288], replicated
- g_proj: float32 [96, 96], replicated
- g_rel: float32 [3, 2197], replicated
- gain_gradient: float32 [96], replicated
- g_shift: float32 [96], replicated
All inputs are finite; a program needn't handle non-finite values.
Results may differ from a plain program's by a relative error of at most 0.011.
Values may be sent and summed in bfloat16 or wider, within the bound.
A program may use at most 192 MiB of HBM per device.

v0:
```python
import jax
import jax.numpy as jnp
from jax import lax
from jax.sharding import PartitionSpec as P

WIN = 7
SHIFT = 3


def shifted(block, axis, distance):
    devices = range(lax.axis_size(axis))
    route = [((i - distance) % len(devices), i) for i in devices]
    return lax.ppermute(block, axis, route)


def in_one(arrays, axis):
    ends = [0]
    for a in arrays:
        ends.append(ends[-1] + a.size)
    so_far = lax.psum(jnp.concatenate([a.ravel() for a in arrays]), axis)
    return tuple((so_far[b:e].reshape(a.shape) for a, b, e in zip(arrays, ends, ends[1:])))


def offset_ones(span):
    first = jnp.arange(span)[:, None, None]
    second = jnp.arange(span)[None, :, None]
    third = jnp.arange(2 * span - 1)[None, None, :]
    return (first - second + span - 1 == third).astype(jnp.float32)


def expand_table(table, span):
    exact = lax.Precision.HIGHEST
    ones = offset_ones(span)
    width = 2 * span - 1
    heads = table.shape[0]
    cube = table.reshape(heads, width, width, width)
    section = jnp.einsum("hxyz,cCz->hxycC", cube, ones, precision=exact)
    section = jnp.einsum("hxycC,bBy->hxbcBC", section, ones, precision=exact)
    section = jnp.einsum("hxbcBC,aAx->habcABC", section, ones, precision=exact)
    return section.reshape(heads, span**3, span**3)


def fold_table(pairs, span):
    exact = lax.Precision.HIGHEST
    ones = offset_ones(span)
    heads = pairs.shape[0]
    grid = pairs.reshape(heads, span, span, span, span, span, span)
    section = jnp.einsum("habcABC,aAx->hxbcBC", grid, ones, precision=exact)
    section = jnp.einsum("hxbcBC,bBy->hxycC", section, ones, precision=exact)
    section = jnp.einsum("hxycC,cCz->hxyz", section, ones, precision=exact)
    return section.reshape(heads, -1)


def region_label(start, cells, count):
    places = start + jnp.arange(cells)
    return jnp.where(places < count - WIN, 0, jnp.where(places < count - SHIFT, 1, 2)).astype(
        jnp.int32
    )


def to_windows(array):
    first, second, third = array.shape[:3]
    rest = array.shape[3:]
    shaped = array.reshape((first // WIN, WIN, second // WIN, WIN, third // WIN, WIN) + rest)
    order = (0, 2, 4, 1, 3, 5) + tuple(range(6, 6 + len(rest)))
    return shaped.transpose(order).reshape((-1, WIN**3) + rest)


def from_windows(array, first, second, third):
    feats = array.shape[-1]
    shaped = array.reshape(first // WIN, second // WIN, third // WIN, WIN, WIN, WIN, feats)
    return shaped.transpose(0, 3, 1, 4, 2, 5, 6).reshape(first, second, third, feats)


def forward_depth(pair):
    arrived = shifted(pair[:, :SHIFT], "gx", -1)
    return jnp.concatenate([pair[:, SHIFT:], arrived], 1)


def forward_height(pair):
    arrived = shifted(pair[:, :, :SHIFT], "gy", -1)
    return jnp.concatenate([pair[:, :, SHIFT:], arrived], 2)


def forward_width(pair):
    arrived = shifted(pair[:, :, :, :SHIFT], "gz", -1)
    return jnp.concatenate([pair[:, :, :, SHIFT:], arrived], 3)


def backward_depth(field):
    edge = field.shape[0] - SHIFT
    arrived = shifted(field[edge:], "gx", 1)
    return jnp.concatenate([arrived, field[:edge]], 0)


def backward_height(field):
    edge = field.shape[1] - SHIFT
    arrived = shifted(field[:, edge:], "gy", 1)
    return jnp.concatenate([arrived, field[:, :edge]], 1)


def backward_width(field):
    edge = field.shape[2] - SHIFT
    arrived = shifted(field[:, :, edge:], "gz", 1)
    return jnp.concatenate([arrived, field[:, :, :edge]], 2)


def window_pass(ln_w, dy_w, lab_w, w_qkv, b_qkv, w_proj, bias_full):
    f32 = jnp.float32
    bf16 = jnp.bfloat16
    group, tok, feats = ln_w.shape
    heads = bias_full.shape[0]
    hdim = feats // heads
    scale = hdim ** (-0.5)
    qkv = jnp.einsum("gtc,cf->gtf", ln_w, w_qkv, preferred_element_type=f32) + b_qkv
    qkv = qkv.astype(bf16).reshape(group, tok, 3, heads, hdim)
    query = qkv[:, :, 0].transpose(0, 2, 1, 3)
    keys = qkv[:, :, 1].transpose(0, 2, 1, 3)
    values = qkv[:, :, 2].transpose(0, 2, 1, 3)
    scores = (
        jnp.einsum("ghid,ghjd->ghij", query, keys, preferred_element_type=f32) * scale
        + bias_full[None]
    )
    allowed = (lab_w[:, :, None] == lab_w[:, None, :])[:, None]
    scores = jnp.where(allowed, scores, f32(-1e30))
    top = jnp.max(scores, -1, keepdims=True)
    expo = jnp.exp(scores - top)
    probs = expo / jnp.sum(expo, -1, keepdims=True)
    probs_b = probs.astype(bf16)
    attended = jnp.einsum("ghij,ghjd->ghid", probs_b, values, preferred_element_type=f32)
    attended = attended.transpose(0, 2, 1, 3).reshape(group, tok, feats).astype(bf16)
    grad_att = jnp.einsum("gtc,fc->gtf", dy_w, w_proj, preferred_element_type=f32).astype(bf16)
    proj_part = jnp.einsum("gtf,gtc->fc", attended, dy_w, preferred_element_type=f32)
    grad_heads = grad_att.reshape(group, tok, heads, hdim).transpose(0, 2, 1, 3)
    grad_probs = jnp.einsum("ghid,ghjd->ghij", grad_heads, values, preferred_element_type=f32)
    grad_v = jnp.einsum("ghij,ghid->ghjd", probs_b, grad_heads, preferred_element_type=f32)
    grad_scores = probs * (grad_probs - jnp.sum(probs * grad_probs, -1, keepdims=True))
    rel_part = jnp.sum(grad_scores, 0)
    scores_b = grad_scores.astype(bf16)
    grad_q = jnp.einsum("ghij,ghjd->ghid", scores_b, keys, preferred_element_type=f32) * scale
    grad_k = jnp.einsum("ghij,ghid->ghjd", scores_b, query, preferred_element_type=f32) * scale
    grad_qkv = (
        jnp.stack([grad_q, grad_k, grad_v], 1)
        .transpose(0, 3, 1, 2, 4)
        .reshape(group, tok, 3 * feats)
    )
    bias_part = jnp.sum(grad_qkv, (0, 1))
    qkv_b = grad_qkv.astype(bf16)
    weight_part = jnp.einsum("gtc,gtf->cf", ln_w, qkv_b, preferred_element_type=f32)
    grad_in = jnp.einsum("gtf,cf->gtc", qkv_b, w_qkv, preferred_element_type=f32)
    return (grad_in, (weight_part, bias_part, proj_part, rel_part))


def shards(inputs, d_out, layer_norm_gain, layer_norm_bias, w_qkv, b_qkv, w_proj, rel_bias):
    f32 = jnp.float32
    cells_x, cells_y, cells_z, feats = inputs.shape
    tok = WIN**3
    heads = rel_bias.shape[0]
    xf = inputs.astype(f32)
    centered_input = xf - jnp.mean(xf, -1, keepdims=True)
    inverse_deviation = lax.rsqrt(
        jnp.mean(centered_input * centered_input, -1, keepdims=True) + 1e-05
    )
    normalized_input = centered_input * inverse_deviation
    normalized_tokens = (normalized_input * layer_norm_gain + layer_norm_bias).astype(jnp.bfloat16)
    moved_pair = jnp.stack([normalized_tokens, d_out])
    forward_steps = (forward_depth, forward_height, forward_width)
    backward_steps = (backward_depth, backward_height, backward_width)
    for advance in forward_steps:
        moved_pair = advance(moved_pair)
    label_x = region_label(lax.axis_index("gx") * cells_x, cells_x, cells_x * lax.axis_size("gx"))
    label_y = region_label(lax.axis_index("gy") * cells_y, cells_y, cells_y * lax.axis_size("gy"))
    label_z = region_label(lax.axis_index("gz") * cells_z, cells_z, cells_z * lax.axis_size("gz"))
    labels = label_x[:, None, None] * 9 + label_y[None, :, None] * 3 + label_z[None, None, :]
    bias_full = expand_table(rel_bias, WIN)
    group = cells_y // WIN * (cells_z // WIN)
    win_ln = to_windows(moved_pair[0]).reshape(-1, group, tok, feats)
    win_dy = to_windows(moved_pair[1]).reshape(-1, group, tok, feats)
    win_lab = to_windows(labels).reshape(-1, group, tok)

    def step(carry, item):
        grad_in, parts = window_pass(item[0], item[1], item[2], w_qkv, b_qkv, w_proj, bias_full)
        return (tuple((total + part for total, part in zip(carry, parts))), grad_in)

    start = (
        jnp.zeros((feats, 3 * feats), f32),
        jnp.zeros((3 * feats,), f32),
        jnp.zeros((feats, feats), f32),
        jnp.zeros((heads, tok, tok), f32),
    )
    sums, grad_win = lax.scan(step, start, (win_ln, win_dy, win_lab))
    normalized_output_gradient = from_windows(
        grad_win.reshape(-1, tok, feats), cells_x, cells_y, cells_z
    )
    for retreat in backward_steps:
        normalized_output_gradient = retreat(normalized_output_gradient)
    normalized_gradient = normalized_output_gradient * layer_norm_gain
    input_gradient_norm = inverse_deviation * (
        normalized_gradient
        - jnp.mean(normalized_gradient, -1, keepdims=True)
        - normalized_input * jnp.mean(normalized_gradient * normalized_input, -1, keepdims=True)
    )
    d_x = (d_out.astype(f32) + input_gradient_norm).astype(jnp.bfloat16)
    rel_local = fold_table(sums[3], WIN)
    local_gain = jnp.sum(normalized_output_gradient * normalized_input, (0, 1, 2))
    shift_local = jnp.sum(normalized_output_gradient, (0, 1, 2))
    totals = in_one(
        (sums[0], sums[1], sums[2], rel_local, local_gain, shift_local), ("gx", "gy", "gz")
    )
    count = (
        cells_x
        * cells_y
        * cells_z
        * lax.axis_size("gx")
        * lax.axis_size("gy")
        * lax.axis_size("gz")
    )
    inverse_width_factor = float(count) ** (-0.5)
    return (
        d_x,
        totals[0] * inverse_width_factor,
        totals[1] * inverse_width_factor,
        totals[2] * inverse_width_factor,
        totals[3] * inverse_width_factor,
        totals[4] * inverse_width_factor,
        totals[5] * inverse_width_factor,
    )


def solution(mesh):
    placed = (P("gx", "gy", "gz", None), P("gx", "gy", "gz", None), P(), P(), P(), P(), P(), P())
    return jax.shard_map(
        shards,
        mesh=mesh,
        in_specs=placed,
        out_specs=(P("gx", "gy", "gz", None), P(), P(), P(), P(), P(), P()),
        check_vma=False,
    )
```

profile of v0, /device:TPU:1, one launch (start us, length us, event | category | flops | bytes accessed | tf_op | source)
XLA Modules:
  0.0 693.7 jit_solution(11061455618265051562)
XLA Ops:
  15.1 3.6 collective-permute-start
  20.4 9.5 %convolution_bitcast_fusion.5 = f32[3,13,7,7,7,7]{1,2,5,3,0,4:T(8,128)S(1)} fusion(f32[3,13,13,7,7]{2,3,1,0,4:T(8,128)S(1)} %convolution_bitcast_fusion.7, s32[7,7]{0,1:T(8,128)S(1)} %subtract_add_fusion), kind=kOutput, calls=%fused_computation.96 | convolution fusion | flops 14608321 | bytes 474124 | tf_op jit(solution)/shard_map/hxycC,bBy->hxbcBC/dot_general | solution.py:38
  30.9 18.5 %collective-permute-start.1 = (bf16[2,28,3,7,96]{4,3,2,1,0:T(8,128)(2,1)S(1)}, bf16[2,28,3,7,96]{4,3,2,1,0:T(8,128)(2,1)S(1)}, u32[]{:S(2)}, u32[]{:S(2)}) collective-permute-start(bf16[2,28,3,7,96]{4,3,2,1,0:T(8,128)(2,1)S(1)} %pad_maximum_fusion.5), channel_id=1, source_target_pairs={{8,0},{16,8},{24,16},{0,24},{9,1},{17,9},{25,17},{1,25},{10,2},{18... | collective-permute-start | bytes 677384 | tf_op jit(solution)/shard_map/ppermute | solution.py:13
  50.3 5.2 collective-permute-done.1
  59.2 5.9 collective-permute-start.2
  65.2 71.1 %convolution_bitcast_fusion.3 = f32[3,7,7,7,7,7,7]{6,4,5,3,2,0,1:T(8,128)} fusion(f32[3,13,7,7,7,7]{1,2,5,3,0,4:T(8,128)S(1)} %convolution_bitcast_fusion.5, pred[7,7,13,1,1,1,1]{2,0,1,6,5,4,3:T(8,128)(4,1)S(1)} %fusion.73), kind=kOutput, calls=%fused_computation.61 | convolution fusion | flops 55059736 | bytes 1786981 | tf_op jit(solution)/shard_map/hxbcBC,aAx->habcABC/dot_general | solution.py:39
  136.3 59.5 %copy.82 = f32[3,7,7,7,7,7,7]{3,2,1,6,5,4,0:T(8,128)} copy(f32[3,7,7,7,7,7,7]{6,4,5,3,2,0,1:T(8,128)} %convolution_bitcast_fusion.3) | data formatting | bytes 2823576
  195.9 21.0 %add.230 = f32[3,343,343]{1,2,0:T(8,128)} reshape(f32[3,7,7,7,7,7,7]{3,2,1,6,5,4,0:T(8,128)} %copy.82) | data formatting | bytes 2823576 | tf_op jit(solution)/shard_map/while/body/eval_jaxpr/add | solution.py:121
  233.2 134.0 %while.20 = (s32[]{:T(128)}, f32[96,288]{1,0:T(8,128)}, f32[288]{0:T(512)S(1)}, f32[96,96]{1,0:T(8,128)S(1)}, f32[3,343,343]{1,2,0:T(8,128)}, /*index=5*/f32[4,4...) while((s32[]{:T(128)}, f32[96,288]{1,0:T(8,128)}, ...), condition=%wide.wide.region_8.9_spmd.clone, body=%wide.wide.region_2.8_spmd.clone.sunk | while | flops 848489408 | bytes 107633568 | solution.py:191
  235.7 7.0 %fusion.174 = (f32[4,3,343]{2,1,0:T(4,128)S(1)}, f32[4,3,343,343]{2,3,1,0:T(8,128)}) fusion(f32[3,343,343]{1,2,0:T(8,128)} %get-tuple-element.420, pred[4,343,343]{1,2,0:T(8,128)(4,1)} %broadcast_compare_fusion.3, bf16[4,343,3,3,32]{1,4,3,2,0:T(8,128)(2,1)S(1)} %bitcast.281), kind=kOutput, calls=%fused_computation.146.clone.clone.1 | convolution fusion | flops 97413720 | bytes 8135824 | tf_op jit(solution)/shard_map/while/body/eval_jaxpr/sub | solution.py:127
  243.0 6.9 multiply_reduce_fusion.4
  249.9 4.2 fusion.176
  268.1 7.0 %fusion.174 = (f32[4,3,343]{2,1,0:T(4,128)S(1)}, f32[4,3,343,343]{2,3,1,0:T(8,128)}) fusion(f32[3,343,343]{1,2,0:T(8,128)} %get-tuple-element.420, pred[4,343,343]{1,2,0:T(8,128)(4,1)} %broadcast_compare_fusion.3, bf16[4,343,3,3,32]{1,4,3,2,0:T(8,128)(2,1)S(1)} %bitcast.281), kind=kOutput, calls=%fused_computation.146.clone.clone.1 | convolution fusion | flops 97413720 | bytes 8135824 | tf_op jit(solution)/shard_map/while/body/eval_jaxpr/sub | solution.py:127
  275.3 6.9 multiply_reduce_fusion.4
  282.2 4.2 fusion.176
  301.9 7.0 %fusion.174 = (f32[4,3,343]{2,1,0:T(4,128)S(1)}, f32[4,3,343,343]{2,3,1,0:T(8,128)}) fusion(f32[3,343,343]{1,2,0:T(8,128)} %get-tuple-element.420, pred[4,343,343]{1,2,0:T(8,128)(4,1)} %broadcast_compare_fusion.3, bf16[4,343,3,3,32]{1,4,3,2,0:T(8,128)(2,1)S(1)} %bitcast.281), kind=kOutput, calls=%fused_computation.146.clone.clone.1 | convolution fusion | flops 97413720 | bytes 8135824 | tf_op jit(solution)/shard_map/while/body/eval_jaxpr/sub | solution.py:127
  309.1 6.9 multiply_reduce_fusion.4
  316.1 4.2 fusion.176
  329.5 3.6 fusion.182
  335.7 6.9 %fusion.174 = (f32[4,3,343]{2,1,0:T(4,128)S(1)}, f32[4,3,343,343]{2,3,1,0:T(8,128)}) fusion(f32[3,343,343]{1,2,0:T(8,128)} %get-tuple-element.420, pred[4,343,343]{1,2,0:T(8,128)(4,1)} %broadcast_compare_fusion.3, bf16[4,343,3,3,32]{1,4,3,2,0:T(8,128)(2,1)S(1)} %bitcast.281), kind=kOutput, calls=%fused_computation.146.clone.clone.1 | convolution fusion | flops 97413720 | bytes 8135824 | tf_op jit(solution)/shard_map/while/body/eval_jaxpr/sub | solution.py:127
  342.9 6.9 multiply_reduce_fusion.4
  349.9 4.2 fusion.176
  373.5 20.0 %reshape.174 = f32[3,7,7,7,7,7,7]{3,2,1,6,5,4,0:T(8,128)} reshape(f32[3,343,343]{1,2,0:T(8,128)S(1)} %copy-done) | data formatting | bytes 2823576 | tf_op jit(solution)/shard_map/reshape | solution.py:47
  393.5 59.7 %copy.88 = f32[3,7,7,7,7,7,7]{1,6,4,5,3,2,0:T(8,128)} copy(f32[3,7,7,7,7,7,7]{3,2,1,6,5,4,0:T(8,128)} %reshape.174) | data formatting | bytes 2823576 | tf_op jit(solution)/shard_map/reshape | solution.py:47
  454.0 25.1 %convolution_bitcast_fusion.4 = f32[3,13,7,7,7,7]{1,5,4,3,2,0:T(8,128)} fusion(f32[3,7,7,7,7,7,7]{1,6,4,5,3,2,0:T(8,128)} %copy.88, s32[7,7]{0,1:T(8,128)S(1)} %copy-done.23), kind=kOutput, calls=%fused_computation.95 | convolution fusion | flops 55060372 | bytes 1786540 | tf_op jit(solution)/shard_map/habcABC,aAx->hxbcBC/dot_general | solution.py:48
  479.1 12.7 %copy.89 = f32[3,13,7,7,7,7]{2,3,4,5,1,0:T(8,128)} copy(f32[3,13,7,7,7,7]{1,5,4,3,2,0:T(8,128)} %convolution_bitcast_fusion.4) | data formatting | bytes 749112 | tf_op jit(solution)/shard_map/habcABC,aAx->hxbcBC/transpose | solution.py:48
  496.7 5.4 convolution_bitcast_fusion.6
  503.7 4.0 slice_reduce_fusion
  507.6 22.6 %collective-permute-done.5 = f32[28,28,3,96]{3,1,2,0:T(8,128)S(1)} collective-permute-done((f32[28,28,3,96]{3,1,2,0:T(8,128)}, f32[28,28,3,96]{3,1,2,0:T(8,128)S(1)}, u32[]{:S(2)}, u32[]{:S(2)}) %collective-permute-start.5) | collective-permute-done | bytes 903200 | tf_op jit(solution)/shard_map/ppermute | solution.py:13
  532.0 6.0 fusion.61
  540.9 8.0 %fusion.60 = bf16[28,28,7,96]{3,2,1,0:T(8,128)(2,1)} fusion(bf16[28,28,7,96]{3,2,1,0:T(8,128)(2,1)S(1)} %copy-done.2, bf16[28,28,7,96]{3,2,1,0:T(8,128)(2,1)S(1)} %copy-done.6, f32[28,28,7]{2,1,0:T(8,128)S(1)} %broadcast_multiply_fusion, f32[28,28,7]{2,1,0:T(8,128)S(1)} %broadcast_multiply_fusion.1, f32[96]{0:T(128)S(1)} %copy-done.27, ...), kind=kLoop, calls=%fused_computation.78 | loop fusion | flops 6322176 | bytes 5356672 | tf_op jit(solution)/shard_map/convert_element_type | solution.py:203
  548.9 130.4 %all-reduce.2.cloned.1.call-done = f32[43935]{0:T(1024)} async-done(((f32[43935]{0:T(1024)}), f32[43935]{0:T(1024)}) %all-reduce.2.cloned.1.call-update) | async-done | bytes 175756 | tf_op jit(solution)/shard_map/psum | solution.py:20
  (236 shorter events, 114.1 us)
Async XLA Ops:
  7.2 672.1 %all-reduce.2.cloned.1.call-start = ((), (), s32[]{:S(2)}) async-start(), calls=%async_computation | async-start | bytes 352256 | tf_op jit(solution)/shard_map/psum | solution.py:20
  15.1 15.7 %collective-permute-start = (bf16[2,3,28,7,96]{4,3,2,1,0:T(8,128)(2,1)S(1)}, bf16[2,3,28,7,96]{4,3,2,1,0:T(8,128)(2,1)S(1)}, u32[]{:S(2)}, u32[]{:S(2)}) collective-permute-start(bf16[2,3,28,7,96]{4,3,2,1,0:T(8,128)(2,1)S(1)} %pad_maximum_fusion.6), channel_id=1, source_target_pairs={{32,0},{64,32},{96,64},{0,96},{33,1},{65,33},{97,65},{1,97},{34,2}... | collective-permute-start | bytes 677384 | tf_op jit(solution)/shard_map/ppermute | solution.py:13
  18.7 30.7 %copy-start.22 = (s32[7,7]{0,1:T(8,128)}, s32[7,7]{0,1:T(8,128)S(1)}, u32[]{:S(2)}) copy-start(s32[7,7]{0,1:T(8,128)S(1)} %subtract_add_fusion) | copy-start | bytes 592
  19.0 11.0 %copy-start.12 = (bf16[1,28,28,7,96]{4,3,2,1,0:T(8,128)(2,1)S(1)}, bf16[1,28,28,7,96]{4,3,2,1,0:T(8,128)(2,1)}, u32[]{:S(2)}) copy-start(bf16[1,28,28,7,96]{4,3,2,1,0:T(8,128)(2,1)} %copy-done.11) | copy-start | bytes 3161092
  30.9 24.6 %collective-permute-start.1 = (bf16[2,28,3,7,96]{4,3,2,1,0:T(8,128)(2,1)S(1)}, bf16[2,28,3,7,96]{4,3,2,1,0:T(8,128)(2,1)S(1)}, u32[]{:S(2)}, u32[]{:S(2)}) collective-permute-start(bf16[2,28,3,7,96]{4,3,2,1,0:T(8,128)(2,1)S(1)} %pad_maximum_fusion.5), channel_id=1, source_target_pairs={{8,0},{16,8},{24,16},{0,24},{9,1},{17,9},{25,17},{1,25},{10,2},{18... | collective-permute-start | bytes 677384 | tf_op jit(solution)/shard_map/ppermute | solution.py:13
  59.2 161.3 %collective-permute-start.2 = (bf16[2,28,28,3,96]{4,0,3,2,1:T(2,128)(2,1)}, bf16[2,28,28,3,96]{4,0,3,2,1:T(2,128)(2,1)}, u32[]{:S(2)}, u32[]{:S(2)}) collective-permute-start(bf16[2,28,28,3,96]{4,0,3,2,1:T(2,128)(2,1)} %copy.74), channel_id=1, source_target_pairs={{1,0},{2,1},{3,2},{4,3},{5,4},{6,5},{7,6},{0,7},{9,8},{10,9},{11,1... | collective-permute-start | bytes 2709512 | tf_op jit(solution)/shard_map/ppermute | solution.py:13
  233.3 9.3 %copy-start.9 = (bf16[4,4,343,96]{2,3,1,0:T(8,128)(2,1)}, bf16[4,4,343,96]{2,3,1,0:T(8,128)(2,1)S(1)}, u32[]{:S(2)}) copy-start(bf16[4,4,343,96]{2,3,1,0:T(8,128)(2,1)S(1)} %get-tuple-element.413) | copy-start | bytes 3161092 | tf_op jit(solution)/shard_map/while
  233.4 9.3 %copy-start.13 = (bf16[4,4,343,96]{2,3,1,0:T(8,128)(2,1)}, bf16[4,4,343,96]{2,3,1,0:T(8,128)(2,1)S(1)}, u32[]{:S(2)}) copy-start(bf16[4,4,343,96]{2,3,1,0:T(8,128)(2,1)S(1)} %get-tuple-element.418) | copy-start | bytes 3161092 | tf_op jit(solution)/shard_map/while
  242.9 6.9 slice-start
  242.9 6.9 slice-start.1
  265.7 9.3 %copy-start.9 = (bf16[4,4,343,96]{2,3,1,0:T(8,128)(2,1)}, bf16[4,4,343,96]{2,3,1,0:T(8,128)(2,1)S(1)}, u32[]{:S(2)}) copy-start(bf16[4,4,343,96]{2,3,1,0:T(8,128)(2,1)S(1)} %get-tuple-element.413) | copy-start | bytes 3161092 | tf_op jit(solution)/shard_map/while
  265.7 9.3 %copy-start.13 = (bf16[4,4,343,96]{2,3,1,0:T(8,128)(2,1)}, bf16[4,4,343,96]{2,3,1,0:T(8,128)(2,1)S(1)}, u32[]{:S(2)}) copy-start(bf16[4,4,343,96]{2,3,1,0:T(8,128)(2,1)S(1)} %get-tuple-element.418) | copy-start | bytes 3161092 | tf_op jit(solution)/shard_map/while
  275.3 6.9 slice-start
  275.3 6.9 slice-start.1
  299.5 9.3 %copy-start.9 = (bf16[4,4,343,96]{2,3,1,0:T(8,128)(2,1)}, bf16[4,4,343,96]{2,3,1,0:T(8,128)(2,1)S(1)}, u32[]{:S(2)}) copy-start(bf16[4,4,343,96]{2,3,1,0:T(8,128)(2,1)S(1)} %get-tuple-element.413) | copy-start | bytes 3161092 | tf_op jit(solution)/shard_map/while
  299.5 9.3 %copy-start.13 = (bf16[4,4,343,96]{2,3,1,0:T(8,128)(2,1)}, bf16[4,4,343,96]{2,3,1,0:T(8,128)(2,1)S(1)}, u32[]{:S(2)}) copy-start(bf16[4,4,343,96]{2,3,1,0:T(8,128)(2,1)S(1)} %get-tuple-element.418) | copy-start | bytes 3161092 | tf_op jit(solution)/shard_map/while
  309.1 6.9 slice-start
  309.1 6.9 slice-start.1
  333.3 9.3 %copy-start.9 = (bf16[4,4,343,96]{2,3,1,0:T(8,128)(2,1)}, bf16[4,4,343,96]{2,3,1,0:T(8,128)(2,1)S(1)}, u32[]{:S(2)}) copy-start(bf16[4,4,343,96]{2,3,1,0:T(8,128)(2,1)S(1)} %get-tuple-element.413) | copy-start | bytes 3161092 | tf_op jit(solution)/shard_map/while
  333.4 9.3 %copy-start.13 = (bf16[4,4,343,96]{2,3,1,0:T(8,128)(2,1)}, bf16[4,4,343,96]{2,3,1,0:T(8,128)(2,1)S(1)}, u32[]{:S(2)}) copy-start(bf16[4,4,343,96]{2,3,1,0:T(8,128)(2,1)S(1)} %get-tuple-element.418) | copy-start | bytes 3161092 | tf_op jit(solution)/shard_map/while
  342.9 6.9 slice-start
  342.9 6.9 slice-start.1
  371.7 81.5 %collective-permute-start.3 = (f32[3,28,7,96]{3,2,1,0:T(8,128)}, f32[3,28,7,96]{3,2,1,0:T(8,128)S(1)}, u32[]{:S(2)}, u32[]{:S(2)}) collective-permute-start(f32[3,28,7,96]{3,2,1,0:T(8,128)} %slice.103), channel_id=1, source_target_pairs={{96,0},{0,32},{32,64},{64,96},{97,1},{1,33},{33,65},{65,97},{98,2}... | collective-permute-start | bytes 677384 | tf_op jit(solution)/shard_map/ppermute | solution.py:13
  393.5 59.7 %copy-start.4 = (f32[25,28,7,96]{3,2,1,0:T(8,128)S(1)}, f32[25,28,7,96]{3,2,1,0:T(8,128)}, u32[]{:S(2)}) copy-start(f32[25,28,7,96]{3,2,1,0:T(8,128)} %slice.104) | copy-start | bytes 5644804
  454.0 37.7 %collective-permute-start.4 = (f32[28,3,7,96]{3,2,1,0:T(8,128)}, f32[28,3,7,96]{3,2,1,0:T(8,128)}, u32[]{:S(2)}, u32[]{:S(2)}) collective-permute-start(f32[28,3,7,96]{3,2,1,0:T(8,128)} %pad_maximum_fusion.4), channel_id=1, source_target_pairs={{24,0},{0,8},{8,16},{16,24},{25,1},{1,9},{9,17},{17,25},{26,2},{2,... | collective-permute-start | bytes 677384 | tf_op jit(solution)/shard_map/ppermute | solution.py:13
  493.3 8.8 %copy-start.15 = (f32[28,28,7,96]{3,2,1,0:T(8,128)}, f32[28,28,7,96]{3,2,1,0:T(8,128)S(1)}, u32[]{:S(2)}) copy-start(f32[28,28,7,96]{3,2,1,0:T(8,128)S(1)} %fusion.63) | copy-start | bytes 6322180
  495.0 8.4 %copy-start.19 = (f32[96,288]{1,0:T(8,128)S(1)}, f32[96,288]{1,0:T(8,128)}, u32[]{:S(2)}) copy-start(f32[96,288]{1,0:T(8,128)} %get-tuple-element.79) | copy-start | bytes 331780
  495.0 35.2 %collective-permute-start.5 = (f32[28,28,3,96]{3,1,2,0:T(8,128)}, f32[28,28,3,96]{3,1,2,0:T(8,128)S(1)}, u32[]{:S(2)}, u32[]{:S(2)}) collective-permute-start(f32[28,28,3,96]{3,1,2,0:T(8,128)} %copy.86), channel_id=1, source_target_pairs={{7,0},{0,1},{1,2},{2,3},{3,4},{4,5},{5,6},{6,7},{15,8},{8,9},{9,10... | collective-permute-start | bytes 2709512 | tf_op jit(solution)/shard_map/ppermute | solution.py:13
  503.6 27.9 %copy-start.2 = (bf16[28,28,7,96]{3,2,1,0:T(8,128)(2,1)S(1)}, bf16[28,28,7,96]{3,2,1,0:T(8,128)(2,1)}, u32[]{:S(2)}) copy-start(bf16[28,28,7,96]{3,2,1,0:T(8,128)(2,1)} %param.10) | copy-start | bytes 3161092
  503.6 27.9 %copy-start.27 = (f32[96]{0:T(128)S(1)}, f32[96]{0:T(128)}, u32[]{:S(2)}) copy-start(f32[96]{0:T(128)} %param.12) | copy-start | bytes 1156
  531.5 6.4 copy-start.8
  532.0 8.9 %copy-start.6 = (bf16[28,28,7,96]{3,2,1,0:T(8,128)(2,1)S(1)}, bf16[28,28,7,96]{3,2,1,0:T(8,128)(2,1)}, u32[]{:S(2)}) copy-start(bf16[28,28,7,96]{3,2,1,0:T(8,128)(2,1)} %param.11) | copy-start | bytes 3161092
  (24 other events, 86.8 us)
Sparse Core Ops, SparseCore 0:
  538.9 140.4 all-reduce.1
where the time goes:
time: 702 us; the launch traced here: 694 us
  matrix products  211 us (30%)
  local copies, waits for them, and re-layouts  207 us (29%)
  waiting for transfers between devices  158 us (23%)
  other arithmetic  74.5 us (11%)
  starting transfers between devices  28.3 us (4%)
  between operations  14.8 us (2%)
    psum x1, waiting for transfers between devices, in_one(): so_far = lax.psum(jnp.concatenate([a.ravel() for a in arrays]), axis)  130 us
    reshape x2, local copies, waits for them, and re-layouts, fold_table(): grid = pairs.reshape(heads, span, span, span, span, span, span)  79.7 us
    dot_general x1, matrix products, expand_table(): section = jnp.einsum('hxbcBC,aAx->habcABC', section, ones, precision=exact)  71.1 us
    unnamed x53, local copies, waits for them, and re-layouts  67.9 us
    ppermute x6, starting transfers between devices, shifted(): return lax.ppermute(block, axis, route)  28.3 us
    sub x4, matrix products, window_pass(): expo = jnp.exp(scores - top)  27.8 us
    ppermute x6, waiting for transfers between devices, shifted(): return lax.ppermute(block, axis, route)  27.8 us
    dot_general x4, matrix products, window_pass(): jnp.einsum('ghid,ghjd->ghij', grad_heads, values, preferred_element_type=...  27.7 us
  transfers between devices with their start and end apart: 7, of which 3 were waited for; matrix products, arithmetic and copies ran while one was open for 44% of the time, Pallas kernels for 0%

commit v1 on v0

--- a/solution.py
+++ b/solution.py
@@ -17,7 +17,7 @@
     ends = [0]
     for a in arrays:
         ends.append(ends[-1] + a.size)
-    so_far = lax.psum(jnp.concatenate([a.ravel() for a in arrays]), axis)
+    so_far = jnp.sum(lax.all_gather(jnp.concatenate([a.ravel() for a in arrays]), axis), axis=0)
     return tuple((so_far[b:e].reshape(a.shape) for a, b, e in zip(arrays, ends, ends[1:])))
 
 

time: 702 us -> 832 us (1.19)
  waiting for transfers between devices: 158 us -> 244 us
  local copies, waits for them, and re-layouts: 207 us -> 248 us
    unnamed x1 -> x2, waiting for transfers between devices: 0.02 us -> 214 us
    psum x1 -> x0, waiting for transfers between devices: 130 us -> none  [in_one(): so_far = lax.psum(jnp.concatenate([a.ravel() for a in arrays]), axis)]
    all_gather x0 -> x1, local copies, waits for them, and re-layouts: none -> 27.6 us  [in_one(): lax.all_gather(jnp.concatenate([a.ravel() for a in arrays]), axis)]
    unnamed x53 -> x63, local copies, waits for them, and re-layouts: 67.9 us -> 79.1 us
    reduce_sum x0 -> x1, other arithmetic: none -> 8.48 us  [in_one(): jnp.sum(lax.all_gather(jnp.concatenate([a.ravel() for a in arrays]), axis...]
  transfers between devices with their start and end apart: 7 -> 7, of which waited for: 3 -> 3; matrix products, arithmetic and copies ran while one was open for 44% -> 37% of each run, Pallas kernels for 0% -> 0%
where the time goes in v1:
time: 832 us; the launch traced here: 824 us
  local copies, waits for them, and re-layouts  248 us (30%)
  waiting for transfers between devices  244 us (29%)
  matrix products  211 us (25%)
  other arithmetic  77.8 us (9%)
  starting transfers between devices  28.6 us (3%)
  between operations  14.8 us (2%)
    unnamed x2, waiting for transfers between devices  214 us
    reshape x2, local copies, waits for them, and re-layouts, fold_table(): grid = pairs.reshape(heads, span, span, span, span, span, span)  79.5 us
    unnamed x63, local copies, waits for them, and re-layouts  79.1 us
    dot_general x1, matrix products, expand_table(): section = jnp.einsum('hxbcBC,aAx->habcABC', section, ones, precision=exact)  71.1 us
    ppermute x6, waiting for transfers between devices, shifted(): return lax.ppermute(block, axis, route)  29.2 us
    ppermute x6, starting transfers between devices, shifted(): return lax.ppermute(block, axis, route)  28.5 us
    sub x4, matrix products, window_pass(): expo = jnp.exp(scores - top)  27.8 us
    dot_general x4, matrix products, window_pass(): jnp.einsum('ghid,ghjd->ghij', grad_heads, values, preferred_element_type=...  27.7 us
  transfers between devices with their start and end apart: 7, of which 3 were waited for; matrix products, arithmetic and copies ran while one was open for 37% of the time, Pallas kernels for 0%

profile of v1, /device:TPU:1, one launch (start us, length us, event | category | flops | bytes accessed | tf_op | source)
XLA Modules:
  0.0 823.8 jit_solution(8904188467669235827)
XLA Ops:
  20.4 9.5 %convolution_bitcast_fusion.5 = f32[3,13,7,7,7,7]{1,2,5,3,0,4:T(8,128)S(1)} fusion(f32[3,13,13,7,7]{2,3,1,0,4:T(8,128)S(1)} %convolution_bitcast_fusion.7, s32[7,7]{0,1:T(8,128)S(1)} %subtract_add_fusion), kind=kOutput, calls=%fused_computation.96 | convolution fusion | flops 14608321 | bytes 474124 | tf_op jit(solution)/shard_map/hxycC,bBy->hxbcBC/dot_general | solution.py:38
  30.9 18.6 %collective-permute-start.1 = (bf16[2,28,3,7,96]{4,3,2,1,0:T(8,128)(2,1)S(1)}, bf16[2,28,3,7,96]{4,3,2,1,0:T(8,128)(2,1)S(1)}, u32[]{:S(2)}, u32[]{:S(2)}) collective-permute-start(bf16[2,28,3,7,96]{4,3,2,1,0:T(8,128)(2,1)S(1)} %pad_maximum_fusion.5), channel_id=1, source_target_pairs={{8,0},{16,8},{24,16},{0,24},{9,1},{17,9},{25,17},{1,25},{10,2},{18... | collective-permute-start | bytes 677384 | tf_op jit(solution)/shard_map/ppermute | solution.py:13
  50.3 5.2 collective-permute-done.1
  59.3 5.9 collective-permute-start.2
  65.2 71.1 %convolution_bitcast_fusion.3 = f32[3,7,7,7,7,7,7]{6,4,5,3,2,0,1:T(8,128)} fusion(f32[3,13,7,7,7,7]{1,2,5,3,0,4:T(8,128)S(1)} %convolution_bitcast_fusion.5, pred[7,7,13,1,1,1,1]{2,0,1,6,5,4,3:T(8,128)(4,1)S(1)} %fusion.73), kind=kOutput, calls=%fused_computation.61 | convolution fusion | flops 55059736 | bytes 1786981 | tf_op jit(solution)/shard_map/hxbcBC,aAx->habcABC/dot_general | solution.py:39
  137.5 59.5 %copy.82 = f32[3,7,7,7,7,7,7]{3,2,1,6,5,4,0:T(8,128)} copy(f32[3,7,7,7,7,7,7]{6,4,5,3,2,0,1:T(8,128)} %convolution_bitcast_fusion.3) | data formatting | bytes 2823576
  197.0 21.0 %add.230 = f32[3,343,343]{1,2,0:T(8,128)} reshape(f32[3,7,7,7,7,7,7]{3,2,1,6,5,4,0:T(8,128)} %copy.82) | data formatting | bytes 2823576 | tf_op jit(solution)/shard_map/while/body/eval_jaxpr/add | solution.py:121
  232.3 133.9 %while.20 = (s32[]{:T(128)}, f32[96,288]{1,0:T(8,128)}, f32[288]{0:T(512)S(1)}, f32[96,96]{1,0:T(8,128)S(1)}, f32[3,343,343]{1,2,0:T(8,128)}, /*index=5*/f32[4,4...) while((s32[]{:T(128)}, f32[96,288]{1,0:T(8,128)}, ...), condition=%wide.wide.region_8.9_spmd.clone, body=%wide.wide.region_2.8_spmd.clone.sunk | while | flops 848489408 | bytes 107633568 | solution.py:191
  234.9 6.9 fusion.174
  242.1 6.9 multiply_reduce_fusion.4
  249.0 4.2 fusion.176
  267.2 6.9 fusion.174
  274.4 6.9 multiply_reduce_fusion.4
  281.4 4.2 fusion.176
  301.0 6.9 fusion.174
  308.2 6.9 multiply_reduce_fusion.4
  315.2 4.2 fusion.176
  334.8 6.9 fusion.174
  342.0 6.9 multiply_reduce_fusion.4
  349.0 4.2 fusion.176
  376.0 19.8 %reshape.174 = f32[3,7,7,7,7,7,7]{3,2,1,6,5,4,0:T(8,128)} reshape(f32[3,343,343]{1,2,0:T(8,128)S(1)} %copy-done) | data formatting | bytes 2823576 | tf_op jit(solution)/shard_map/reshape | solution.py:47
  395.9 59.7 %copy.88 = f32[3,7,7,7,7,7,7]{1,6,4,5,3,2,0:T(8,128)} copy(f32[3,7,7,7,7,7,7]{3,2,1,6,5,4,0:T(8,128)} %reshape.174) | data formatting | bytes 2823576 | tf_op jit(solution)/shard_map/reshape | solution.py:47
  456.3 25.1 %convolution_bitcast_fusion.4 = f32[3,13,7,7,7,7]{1,5,4,3,2,0:T(8,128)} fusion(f32[3,7,7,7,7,7,7]{1,6,4,5,3,2,0:T(8,128)} %copy.88, s32[7,7]{0,1:T(8,128)S(1)} %copy-done.27), kind=kOutput, calls=%fused_computation.95 | convolution fusion | flops 55060372 | bytes 1786540 | tf_op jit(solution)/shard_map/habcABC,aAx->hxbcBC/dot_general | solution.py:48
  481.4 12.6 %copy.89 = f32[3,13,7,7,7,7]{2,3,4,5,1,0:T(8,128)} copy(f32[3,13,7,7,7,7]{1,5,4,3,2,0:T(8,128)} %convolution_bitcast_fusion.4) | data formatting | bytes 749112 | tf_op jit(solution)/shard_map/habcABC,aAx->hxbcBC/transpose | solution.py:48
  499.0 5.4 convolution_bitcast_fusion.6
  508.8 24.0 %collective-permute-done.5 = f32[28,28,3,96]{3,1,2,0:T(8,128)} collective-permute-done((f32[28,28,3,96]{3,1,2,0:T(8,128)}, f32[28,28,3,96]{3,1,2,0:T(8,128)}, u32[]{:S(2)}, u32[]{:S(2)}) %collective-permute-start.5) | collective-permute-done | bytes 903200 | tf_op jit(solution)/shard_map/ppermute | solution.py:13
  537.0 5.0 fusion.61
  542.1 7.7 broadcast.244
  554.6 8.2 fusion.60
  562.8 214.3 %all-reduce.3.cloned.1.call-done = f32[5623680]{0:T(1024)} async-done(((f32[5623680]{0:T(1024)}), f32[5623680]{0:T(1024)}) %all-reduce.3.cloned.1.call-update) | async-done | bytes 22494736
  777.2 27.6 %reshape.175 = f32[128,43935]{1,0:T(8,128)} reshape(f32[5623680]{0:T(1024)} %all-reduce.3.cloned.1.call-done) | data formatting | bytes 44989440 | tf_op jit(solution)/shard_map/all_gather | solution.py:20
  804.8 8.5 %reduce_sum.117 = f32[43935]{0:T(1024)S(1)} reduce(f32[128,43935]{1,0:T(8,128)} %reshape.175, f32[]{:T(128)} %constant.33.clone.1), dimensions={0}, to_apply=%region_14.15 | reduce | flops 5579745 | bytes 22670464 | tf_op jit(solution)/shard_map/reduce_sum | solution.py:20
  (248 shorter events, 127.1 us)
Async XLA Ops:
  7.2 770.0 %all-reduce.3.cloned.1.call-start = ((), (), s32[]{:S(2)}) async-start(), calls=%async_computation | async-start | bytes 44990464
  15.1 15.7 %collective-permute-start = (bf16[2,3,28,7,96]{4,3,2,1,0:T(8,128)(2,1)S(1)}, bf16[2,3,28,7,96]{4,3,2,1,0:T(8,128)(2,1)S(1)}, u32[]{:S(2)}, u32[]{:S(2)}) collective-permute-start(bf16[2,3,28,7,96]{4,3,2,1,0:T(8,128)(2,1)S(1)} %pad_maximum_fusion.6), channel_id=1, source_target_pairs={{32,0},{64,32},{96,64},{0,96},{33,1},{65,33},{97,65},{1,97},{34,2}... | collective-permute-start | bytes 677384 | tf_op jit(solution)/shard_map/ppermute | solution.py:13
  18.7 30.8 %copy-start.26 = (s32[7,7]{0,1:T(8,128)}, s32[7,7]{0,1:T(8,128)S(1)}, u32[]{:S(2)}) copy-start(s32[7,7]{0,1:T(8,128)S(1)} %subtract_add_fusion) | copy-start | bytes 592
  19.0 11.0 %copy-start.12 = (bf16[1,28,28,7,96]{4,3,2,1,0:T(8,128)(2,1)S(1)}, bf16[1,28,28,7,96]{4,3,2,1,0:T(8,128)(2,1)}, u32[]{:S(2)}) copy-start(bf16[1,28,28,7,96]{4,3,2,1,0:T(8,128)(2,1)} %copy-done.11) | copy-start | bytes 3161092
  30.9 24.6 %collective-permute-start.1 = (bf16[2,28,3,7,96]{4,3,2,1,0:T(8,128)(2,1)S(1)}, bf16[2,28,3,7,96]{4,3,2,1,0:T(8,128)(2,1)S(1)}, u32[]{:S(2)}, u32[]{:S(2)}) collective-permute-start(bf16[2,28,3,7,96]{4,3,2,1,0:T(8,128)(2,1)S(1)} %pad_maximum_fusion.5), channel_id=1, source_target_pairs={{8,0},{16,8},{24,16},{0,24},{9,1},{17,9},{25,17},{1,25},{10,2},{18... | collective-permute-start | bytes 677384 | tf_op jit(solution)/shard_map/ppermute | solution.py:13
  59.3 160.4 %collective-permute-start.2 = (bf16[2,28,28,3,96]{4,0,3,2,1:T(2,128)(2,1)}, bf16[2,28,28,3,96]{4,0,3,2,1:T(2,128)(2,1)}, u32[]{:S(2)}, u32[]{:S(2)}) collective-permute-start(bf16[2,28,28,3,96]{4,0,3,2,1:T(2,128)(2,1)} %copy.74), channel_id=1, source_target_pairs={{1,0},{2,1},{3,2},{4,3},{5,4},{6,5},{7,6},{0,7},{9,8},{10,9},{11,1... | collective-permute-start | bytes 2709512 | tf_op jit(solution)/shard_map/ppermute | solution.py:13
  197.0 21.0 %copy-start.24 = (bf16[2,28,3,7,96]{4,3,2,1,0:T(8,128)(2,1)S(1)}, bf16[2,28,3,7,96]{4,3,2,1,0:T(8,128)(2,1)}, u32[]{:S(2)}) copy-start(bf16[2,28,3,7,96]{4,3,2,1,0:T(8,128)(2,1)} %copy-done.23) | copy-start | bytes 677380
  232.5 9.3 %copy-start.9 = (bf16[4,4,343,96]{2,3,1,0:T(8,128)(2,1)}, bf16[4,4,343,96]{2,3,1,0:T(8,128)(2,1)S(1)}, u32[]{:S(2)}) copy-start(bf16[4,4,343,96]{2,3,1,0:T(8,128)(2,1)S(1)} %get-tuple-element.413) | copy-start | bytes 3161092 | tf_op jit(solution)/shard_map/while
  232.5 9.3 %copy-start.13 = (bf16[4,4,343,96]{2,3,1,0:T(8,128)(2,1)}, bf16[4,4,343,96]{2,3,1,0:T(8,128)(2,1)S(1)}, u32[]{:S(2)}) copy-start(bf16[4,4,343,96]{2,3,1,0:T(8,128)(2,1)S(1)} %get-tuple-element.418) | copy-start | bytes 3161092 | tf_op jit(solution)/shard_map/while
  242.1 6.9 slice-start
  242.1 6.9 slice-start.1
  264.8 9.3 %copy-start.9 = (bf16[4,4,343,96]{2,3,1,0:T(8,128)(2,1)}, bf16[4,4,343,96]{2,3,1,0:T(8,128)(2,1)S(1)}, u32[]{:S(2)}) copy-start(bf16[4,4,343,96]{2,3,1,0:T(8,128)(2,1)S(1)} %get-tuple-element.413) | copy-start | bytes 3161092 | tf_op jit(solution)/shard_map/while
  264.9 9.3 %copy-start.13 = (bf16[4,4,343,96]{2,3,1,0:T(8,128)(2,1)}, bf16[4,4,343,96]{2,3,1,0:T(8,128)(2,1)S(1)}, u32[]{:S(2)}) copy-start(bf16[4,4,343,96]{2,3,1,0:T(8,128)(2,1)S(1)} %get-tuple-element.418) | copy-start | bytes 3161092 | tf_op jit(solution)/shard_map/while
  274.4 6.9 slice-start
  274.4 6.9 slice-start.1
  298.6 9.3 %copy-start.9 = (bf16[4,4,343,96]{2,3,1,0:T(8,128)(2,1)}, bf16[4,4,343,96]{2,3,1,0:T(8,128)(2,1)S(1)}, u32[]{:S(2)}) copy-start(bf16[4,4,343,96]{2,3,1,0:T(8,128)(2,1)S(1)} %get-tuple-element.413) | copy-start | bytes 3161092 | tf_op jit(solution)/shard_map/while
  298.7 9.3 %copy-start.13 = (bf16[4,4,343,96]{2,3,1,0:T(8,128)(2,1)}, bf16[4,4,343,96]{2,3,1,0:T(8,128)(2,1)S(1)}, u32[]{:S(2)}) copy-start(bf16[4,4,343,96]{2,3,1,0:T(8,128)(2,1)S(1)} %get-tuple-element.418) | copy-start | bytes 3161092 | tf_op jit(solution)/shard_map/while
  308.2 6.9 slice-start
  308.2 6.9 slice-start.1
  332.5 9.3 %copy-start.9 = (bf16[4,4,343,96]{2,3,1,0:T(8,128)(2,1)}, bf16[4,4,343,96]{2,3,1,0:T(8,128)(2,1)S(1)}, u32[]{:S(2)}) copy-start(bf16[4,4,343,96]{2,3,1,0:T(8,128)(2,1)S(1)} %get-tuple-element.413) | copy-start | bytes 3161092 | tf_op jit(solution)/shard_map/while
  332.5 9.3 %copy-start.13 = (bf16[4,4,343,96]{2,3,1,0:T(8,128)(2,1)}, bf16[4,4,343,96]{2,3,1,0:T(8,128)(2,1)S(1)}, u32[]{:S(2)}) copy-start(bf16[4,4,343,96]{2,3,1,0:T(8,128)(2,1)S(1)} %get-tuple-element.418) | copy-start | bytes 3161092 | tf_op jit(solution)/shard_map/while
  342.0 6.9 slice-start
  342.0 6.9 slice-start.1
  372.5 83.1 %collective-permute-start.3 = (f32[3,28,7,96]{3,2,1,0:T(8,128)}, f32[3,28,7,96]{3,2,1,0:T(8,128)S(1)}, u32[]{:S(2)}, u32[]{:S(2)}) collective-permute-start(f32[3,28,7,96]{3,2,1,0:T(8,128)} %slice.103), channel_id=1, source_target_pairs={{96,0},{0,32},{32,64},{64,96},{97,1},{1,33},{33,65},{65,97},{98,2}... | collective-permute-start | bytes 677384 | tf_op jit(solution)/shard_map/ppermute | solution.py:13
  395.9 59.7 %copy-start.4 = (f32[25,28,7,96]{3,2,1,0:T(8,128)S(1)}, f32[25,28,7,96]{3,2,1,0:T(8,128)}, u32[]{:S(2)}) copy-start(f32[25,28,7,96]{3,2,1,0:T(8,128)} %slice.104) | copy-start | bytes 5644804
  456.3 37.7 %collective-permute-start.4 = (f32[28,3,7,96]{3,2,1,0:T(8,128)}, f32[28,3,7,96]{3,2,1,0:T(8,128)}, u32[]{:S(2)}, u32[]{:S(2)}) collective-permute-start(f32[28,3,7,96]{3,2,1,0:T(8,128)} %pad_maximum_fusion.4), channel_id=1, source_target_pairs={{24,0},{0,8},{8,16},{16,24},{25,1},{1,9},{9,17},{17,25},{26,2},{2,... | collective-permute-start | bytes 677384 | tf_op jit(solution)/shard_map/ppermute | solution.py:13
  495.6 8.8 %copy-start.15 = (f32[28,28,7,96]{3,2,1,0:T(8,128)}, f32[28,28,7,96]{3,2,1,0:T(8,128)S(1)}, u32[]{:S(2)}) copy-start(f32[28,28,7,96]{3,2,1,0:T(8,128)S(1)} %fusion.63) | copy-start | bytes 6322180
  497.3 8.4 %copy-start.22 = (f32[96,288]{1,0:T(8,128)S(1)}, f32[96,288]{1,0:T(8,128)}, u32[]{:S(2)}) copy-start(f32[96,288]{1,0:T(8,128)} %get-tuple-element.79) | copy-start | bytes 331780
  497.3 35.6 %collective-permute-start.5 = (f32[28,28,3,96]{3,1,2,0:T(8,128)}, f32[28,28,3,96]{3,1,2,0:T(8,128)}, u32[]{:S(2)}, u32[]{:S(2)}) collective-permute-start(f32[28,28,3,96]{3,1,2,0:T(8,128)} %copy.86), channel_id=1, source_target_pairs={{7,0},{0,1},{1,2},{2,3},{3,4},{4,5},{5,6},{6,7},{15,8},{8,9},{9,10... | collective-permute-start | bytes 2709512 | tf_op jit(solution)/shard_map/ppermute | solution.py:13
  505.9 31.0 %copy-start.2 = (bf16[28,28,7,96]{3,2,1,0:T(8,128)(2,1)S(1)}, bf16[28,28,7,96]{3,2,1,0:T(8,128)(2,1)}, u32[]{:S(2)}) copy-start(bf16[28,28,7,96]{3,2,1,0:T(8,128)(2,1)} %param.10) | copy-start | bytes 3161092
  506.0 31.0 %copy-start.31 = (f32[96]{0:T(128)S(1)}, f32[96]{0:T(128)}, u32[]{:S(2)}) copy-start(f32[96]{0:T(128)} %param.12) | copy-start | bytes 1156
  508.8 33.1 %copy-start.7 = (f32[28,28,4,96]{3,2,1,0:T(4,128)}, f32[28,28,4,96]{3,2,1,0:T(4,128)S(1)}, u32[]{:S(2)}) copy-start(f32[28,28,4,96]{3,2,1,0:T(4,128)S(1)} %get-tuple-element.213) | copy-start | bytes 3612676
  (28 other events, 101.0 us)
Sparse Core Ops, SparseCore 0:
  552.5 224.6 all-reduce.2
